TPU v7x, 256 devices: a whole 4x4x8 slice. The times are simulated.
256 devices in a mesh: rows: 16 (over z, core), cols: 16 (over y, x).
Axes of the slice: x: 4, y: 4, z: 8, core: 2. Of those that a mesh axis runs over, the one named last changes fastest.
Arguments:
- tensor: float32 [32, 2048, 2048], P(None, 'rows', 'cols'), may hold values from -819200 to 819200
- second_init: float32 [2048, 64], P('cols'), may hold values from -6 to 6
- third_init: float32 [32, 64], replicated, may hold values from -6 to 6
Outputs:
- first: float32 [2048, 64], P('rows')
- second: float32 [2048, 64], P('cols')
- third: float32 [32, 64], replicated
All inputs are finite; a program needn't handle non-finite values.
Results may differ from a plain program's by a relative error of at most 0.0003.
Values sent between devices are 32-bit elements; how exact they have to be, the bound alone decides.
No kernel may reach another device: no remote copies, remote signals or barrier semaphores. Data moves between devices by JAX's collectives and lax.ppermute only.
A program may use at most 64 MiB of HBM per device.

v0:
```python
import jax
import jax.numpy as jnp
from jax import lax
from jax.sharding import PartitionSpec as P

ITERS = 5
EPSILON = 1e-05
HIGHEST = lax.Precision.HIGHEST


def solve_right(rhs_rows, system):
    cholesky_low = jnp.linalg.cholesky(system)
    halfway = lax.linalg.triangular_solve(
        cholesky_low, rhs_rows, left_side=False, lower=True, transpose_a=True
    )
    return lax.linalg.triangular_solve(cholesky_low, halfway, left_side=False, lower=True)


def gram_local(factor):
    return jnp.dot(factor.T, factor, precision=HIGHEST, preferred_element_type=jnp.float32)


def settle(raw_share, total_rows):
    squares = lax.psum(jnp.sum(raw_share * raw_share, axis=0), ("rows", "cols"))
    col_scale = jnp.sqrt(squares / total_rows + EPSILON)
    normed = raw_share / col_scale
    gram_whole = lax.psum(gram_local(normed), ("rows", "cols"))
    return (col_scale, gram_whole)


def per_device(tensor, second_init, third_init):
    rows_here = tensor.shape[1]
    cols_here = tensor.shape[2]
    total_first = rows_here * lax.axis_size("rows")
    total_second = cols_here * lax.axis_size("cols")
    share_first = rows_here // lax.axis_size("cols")
    share_second = cols_here // lax.axis_size("rows")
    start_first = lax.axis_index("cols") * share_first
    start_second = lax.axis_index("rows") * share_second
    col_scale, gram_second = settle(
        lax.dynamic_slice_in_dim(second_init, start_second, share_second, 0), total_second
    )
    second = second_init / col_scale
    third = third_init
    gram_third = gram_local(third)
    first = None
    for sweep_index in range(ITERS):
        contract_first = lax.dot_general(
            second,
            tensor,
            (((0,), (2,)), ((), ())),
            precision=HIGHEST,
            preferred_element_type=jnp.float32,
        )
        system_first = gram_third * gram_second
        gram_first = None
        partial_first = jnp.einsum("rki,kr->ir", contract_first, third, precision=HIGHEST)
        mttkrp_first = lax.psum(partial_first, "cols")
        raw_block = solve_right(mttkrp_first, system_first)
        col_scale, gram_first = settle(
            lax.dynamic_slice_in_dim(raw_block, start_first, share_first, 0), total_first
        )
        carried_first = raw_block / col_scale
        contract_second = lax.dot_general(
            carried_first,
            tensor,
            (((0,), (1,)), ((), ())),
            precision=HIGHEST,
            preferred_element_type=jnp.float32,
        )
        partial_second = jnp.einsum("rkj,kr->jr", contract_second, third, precision=HIGHEST)
        outgoing = partial_second
        summed_second = lax.psum(outgoing, "rows")
        first = carried_first
        system_second = gram_third * gram_first
        raw_block = solve_right(summed_second, system_second)
        raw_part = lax.dynamic_slice_in_dim(raw_block, start_second, share_second, 0)
        col_scale, gram_second = settle(raw_part, total_second)
        carried_second = raw_block / col_scale
        partial_third = jnp.einsum("rkj,jr->kr", contract_second, carried_second, precision=HIGHEST)
        outgoing = partial_third
        summed_third = lax.psum(outgoing, ("rows", "cols"))
        second = carried_second
        third = solve_right(summed_third, gram_first * gram_second)
        gram_third = gram_local(third)
    return (first, second, third)


def solution(mesh):
    return jax.shard_map(
        per_device,
        mesh=mesh,
        in_specs=(P(None, "rows", "cols"), P("cols", None), P()),
        out_specs=(P("rows", None), P("cols", None), P()),
        check_vma=False,
    )
```

profile of v0, /device:TPU:1, one launch (start us, length us, event | category | flops | bytes accessed | tf_op | source)
XLA Modules:
  0.0 2455.2 jit_solution(10629154190226435686)
XLA Ops:
  1.7 81.4 %psum.259 = f32[64]{0:T(128)S(1)} all-reduce(f32[64]{0:T(128)S(1)} %multiply_reduce_fusion.10), channel_id=1, replica_groups=mesh['rows'=16,'cols'=16] {'rows','cols'}, use_global_device_ids=true, to_apply=%region_1.0 | all-reduce | flops 64 | bytes 512 | tf_op jit(solution)/shard_map/psum | solution.py:24
  85.1 72.8 %psum.260 = f32[64,64]{0,1:T(8,128)S(1)} all-reduce(f32[64,64]{0,1:T(8,128)S(1)} %fusion.163), channel_id=1, replica_groups=mesh['rows'=16,'cols'=16] {'rows','cols'}, use_global_device_ids=true, to_apply=%region_2.0 | all-reduce | flops 4096 | bytes 32768 | tf_op jit(solution)/shard_map/psum | solution.py:27
  159.0 5.8 cholesky.239
  166.2 4.9 custom-call.41
  175.8 56.8 %psum.261 = f32[128,64]{0,1:T(8,128)S(1)} all-reduce(f32[128,64]{0,1:T(8,128)S(1)} %bitcast.449), channel_id=1, replica_groups=mesh['rows'=16,'cols'=16] {'cols'}, use_global_device_ids=true, to_apply=%region_5.0 | all-reduce | flops 8192 | bytes 65536 | tf_op jit(solution)/shard_map/psum | solution.py:58
  233.2 86.1 %psum.262 = f32[64]{0:T(128)S(1)} all-reduce(f32[64]{0:T(128)S(1)} %multiply_reduce_fusion.9), channel_id=1, replica_groups=mesh['rows'=16,'cols'=16] {'rows','cols'}, use_global_device_ids=true, to_apply=%region_7.11 | all-reduce | flops 64 | bytes 512 | tf_op jit(solution)/shard_map/psum | solution.py:24
  319.6 73.9 %psum.263 = f32[64,64]{0,1:T(8,128)S(1)} all-reduce(f32[64,64]{0,1:T(8,128)S(1)} %fusion.160), channel_id=1, replica_groups=mesh['rows'=16,'cols'=16] {'rows','cols'}, use_global_device_ids=true, to_apply=%region_8.12 | all-reduce | flops 4096 | bytes 32768 | tf_op jit(solution)/shard_map/psum | solution.py:27
  393.6 5.8 cholesky.250
  408.5 44.1 %psum.264 = f32[128,64]{0,1:T(8,128)S(1)} all-reduce(f32[128,64]{0,1:T(8,128)S(1)} %bitcast.450), channel_id=1, replica_groups=mesh['rows'=16,'cols'=16] {'rows'}, use_global_device_ids=true, to_apply=%region_9.13 | all-reduce | flops 8192 | bytes 65536 | tf_op jit(solution)/shard_map/psum | solution.py:73
  453.3 76.4 %psum.265 = f32[64]{0:T(128)S(1)} all-reduce(f32[64]{0:T(128)S(1)} %multiply_reduce_fusion.8), channel_id=1, replica_groups=mesh['rows'=16,'cols'=16] {'rows','cols'}, use_global_device_ids=true, to_apply=%region_11.15 | all-reduce | flops 64 | bytes 512 | tf_op jit(solution)/shard_map/psum | solution.py:24
  532.2 74.2 %all-reduce.4 = (f32[32,64]{0,1:T(8,128)S(1)}, f32[64,64]{0,1:T(8,128)S(1)}) all-reduce(f32[32,64]{0,1:T(8,128)S(1)} %bitcast.444, f32[64,64]{0,1:T(8,128)S(1)} %fusion.157), channel_id=1, replica_groups=mesh['rows'=16,'cols'=16] {'rows','cols'}, use_global_device_ids=true, to_apply=%region_13.17 | all-reduce | flops 6144 | bytes 49152 | tf_op jit(solution)/shard_map/psum | solution.py:82
  606.5 5.8 cholesky.261
  619.5 5.8 cholesky.272
  635.5 56.8 %psum.268 = f32[128,64]{0,1:T(8,128)S(1)} all-reduce(f32[128,64]{0,1:T(8,128)S(1)} %bitcast.451), channel_id=1, replica_groups=mesh['rows'=16,'cols'=16] {'cols'}, use_global_device_ids=true, to_apply=%region_14.20 | all-reduce | flops 8192 | bytes 65536 | tf_op jit(solution)/shard_map/psum | solution.py:58
  692.9 85.3 %psum.269 = f32[64]{0:T(128)S(1)} all-reduce(f32[64]{0:T(128)S(1)} %multiply_reduce_fusion.7), channel_id=1, replica_groups=mesh['rows'=16,'cols'=16] {'rows','cols'}, use_global_device_ids=true, to_apply=%region_16.22 | all-reduce | flops 64 | bytes 512 | tf_op jit(solution)/shard_map/psum | solution.py:24
  778.5 74.9 %psum.270 = f32[64,64]{0,1:T(8,128)S(1)} all-reduce(f32[64,64]{0,1:T(8,128)S(1)} %fusion.155), channel_id=1, replica_groups=mesh['rows'=16,'cols'=16] {'rows','cols'}, use_global_device_ids=true, to_apply=%region_17.23 | all-reduce | flops 4096 | bytes 32768 | tf_op jit(solution)/shard_map/psum | solution.py:27
  853.5 5.8 cholesky.283
  868.3 43.4 %psum.271 = f32[128,64]{0,1:T(8,128)S(1)} all-reduce(f32[128,64]{0,1:T(8,128)S(1)} %bitcast.452), channel_id=1, replica_groups=mesh['rows'=16,'cols'=16] {'rows'}, use_global_device_ids=true, to_apply=%region_18.24 | all-reduce | flops 8192 | bytes 65536 | tf_op jit(solution)/shard_map/psum | solution.py:73
  912.2 76.4 %psum.272 = f32[64]{0:T(128)S(1)} all-reduce(f32[64]{0:T(128)S(1)} %multiply_reduce_fusion.6), channel_id=1, replica_groups=mesh['rows'=16,'cols'=16] {'rows','cols'}, use_global_device_ids=true, to_apply=%region_20.26 | all-reduce | flops 64 | bytes 512 | tf_op jit(solution)/shard_map/psum | solution.py:24
  991.2 74.1 %all-reduce.3 = (f32[32,64]{0,1:T(8,128)S(1)}, f32[64,64]{0,1:T(8,128)S(1)}) all-reduce(f32[32,64]{0,1:T(8,128)S(1)} %bitcast.445, f32[64,64]{0,1:T(8,128)S(1)} %fusion.152), channel_id=1, replica_groups=mesh['rows'=16,'cols'=16] {'rows','cols'}, use_global_device_ids=true, to_apply=%region_22.28 | all-reduce | flops 6144 | bytes 49152 | tf_op jit(solution)/shard_map/psum | solution.py:82
  1065.4 5.8 cholesky.294
  1078.4 5.8 cholesky.305
  1094.4 56.8 %psum.275 = f32[128,64]{0,1:T(8,128)S(1)} all-reduce(f32[128,64]{0,1:T(8,128)S(1)} %bitcast.453), channel_id=1, replica_groups=mesh['rows'=16,'cols'=16] {'cols'}, use_global_device_ids=true, to_apply=%region_23.29 | all-reduce | flops 8192 | bytes 65536 | tf_op jit(solution)/shard_map/psum | solution.py:58
  1151.8 85.3 %psum.276 = f32[64]{0:T(128)S(1)} all-reduce(f32[64]{0:T(128)S(1)} %multiply_reduce_fusion.5), channel_id=1, replica_groups=mesh['rows'=16,'cols'=16] {'rows','cols'}, use_global_device_ids=true, to_apply=%region_25.31 | all-reduce | flops 64 | bytes 512 | tf_op jit(solution)/shard_map/psum | solution.py:24
  1237.3 74.7 %psum.277 = f32[64,64]{0,1:T(8,128)S(1)} all-reduce(f32[64,64]{0,1:T(8,128)S(1)} %fusion.150), channel_id=1, replica_groups=mesh['rows'=16,'cols'=16] {'rows','cols'}, use_global_device_ids=true, to_apply=%region_26.32 | all-reduce | flops 4096 | bytes 32768 | tf_op jit(solution)/shard_map/psum | solution.py:27
  1312.1 5.8 cholesky.316
  1326.9 43.3 %psum.278 = f32[128,64]{0,1:T(8,128)S(1)} all-reduce(f32[128,64]{0,1:T(8,128)S(1)} %bitcast.454), channel_id=1, replica_groups=mesh['rows'=16,'cols'=16] {'rows'}, use_global_device_ids=true, to_apply=%region_27.33 | all-reduce | flops 8192 | bytes 65536 | tf_op jit(solution)/shard_map/psum | solution.py:73
  1370.9 76.4 %psum.279 = f32[64]{0:T(128)S(1)} all-reduce(f32[64]{0:T(128)S(1)} %multiply_reduce_fusion.4), channel_id=1, replica_groups=mesh['rows'=16,'cols'=16] {'rows','cols'}, use_global_device_ids=true, to_apply=%region_29.35 | all-reduce | flops 64 | bytes 512 | tf_op jit(solution)/shard_map/psum | solution.py:24
  1449.8 74.3 %all-reduce.2 = (f32[32,64]{0,1:T(8,128)S(1)}, f32[64,64]{0,1:T(8,128)S(1)}) all-reduce(f32[32,64]{0,1:T(8,128)S(1)} %bitcast.446, f32[64,64]{0,1:T(8,128)S(1)} %fusion.147), channel_id=1, replica_groups=mesh['rows'=16,'cols'=16] {'rows','cols'}, use_global_device_ids=true, to_apply=%region_31.37 | all-reduce | flops 6144 | bytes 49152 | tf_op jit(solution)/shard_map/psum | solution.py:82
  1524.3 5.8 cholesky.327
  1537.3 5.8 cholesky.338
  1553.2 56.8 %psum.282 = f32[128,64]{0,1:T(8,128)S(1)} all-reduce(f32[128,64]{0,1:T(8,128)S(1)} %bitcast.455), channel_id=1, replica_groups=mesh['rows'=16,'cols'=16] {'cols'}, use_global_device_ids=true, to_apply=%region_32.38 | all-reduce | flops 8192 | bytes 65536 | tf_op jit(solution)/shard_map/psum | solution.py:58
  1610.6 85.3 %psum.283 = f32[64]{0:T(128)S(1)} all-reduce(f32[64]{0:T(128)S(1)} %multiply_reduce_fusion.3), channel_id=1, replica_groups=mesh['rows'=16,'cols'=16] {'rows','cols'}, use_global_device_ids=true, to_apply=%region_34.40 | all-reduce | flops 64 | bytes 512 | tf_op jit(solution)/shard_map/psum | solution.py:24
  1696.2 74.6 %psum.284 = f32[64,64]{0,1:T(8,128)S(1)} all-reduce(f32[64,64]{0,1:T(8,128)S(1)} %fusion.145), channel_id=1, replica_groups=mesh['rows'=16,'cols'=16] {'rows','cols'}, use_global_device_ids=true, to_apply=%region_35.41 | all-reduce | flops 4096 | bytes 32768 | tf_op jit(solution)/shard_map/psum | solution.py:27
  1770.9 5.8 cholesky.349
  1785.8 43.4 %psum.285 = f32[128,64]{0,1:T(8,128)S(1)} all-reduce(f32[128,64]{0,1:T(8,128)S(1)} %bitcast.456), channel_id=1, replica_groups=mesh['rows'=16,'cols'=16] {'rows'}, use_global_device_ids=true, to_apply=%region_36.42 | all-reduce | flops 8192 | bytes 65536 | tf_op jit(solution)/shard_map/psum | solution.py:73
  1829.7 76.4 %psum.286 = f32[64]{0:T(128)S(1)} all-reduce(f32[64]{0:T(128)S(1)} %multiply_reduce_fusion.2), channel_id=1, replica_groups=mesh['rows'=16,'cols'=16] {'rows','cols'}, use_global_device_ids=true, to_apply=%region_38.44 | all-reduce | flops 64 | bytes 512 | tf_op jit(solution)/shard_map/psum | solution.py:24
  1908.7 74.2 %all-reduce.1 = (f32[32,64]{0,1:T(8,128)S(1)}, f32[64,64]{0,1:T(8,128)S(1)}) all-reduce(f32[32,64]{0,1:T(8,128)S(1)} %bitcast.447, f32[64,64]{0,1:T(8,128)S(1)} %fusion.142), channel_id=1, replica_groups=mesh['rows'=16,'cols'=16] {'rows','cols'}, use_global_device_ids=true, to_apply=%region_40.46 | all-reduce | flops 6144 | bytes 49152 | tf_op jit(solution)/shard_map/psum | solution.py:82
  1982.9 5.8 cholesky.360
  1995.9 5.8 cholesky.371
  2011.9 56.8 %psum.289 = f32[128,64]{0,1:T(8,128)S(1)} all-reduce(f32[128,64]{0,1:T(8,128)S(1)} %bitcast.457), channel_id=1, replica_groups=mesh['rows'=16,'cols'=16] {'cols'}, use_global_device_ids=true, to_apply=%region_41.47 | all-reduce | flops 8192 | bytes 65536 | tf_op jit(solution)/shard_map/psum | solution.py:58
  2069.3 85.3 %psum.290 = f32[64]{0:T(128)S(1)} all-reduce(f32[64]{0:T(128)S(1)} %multiply_reduce_fusion.1), channel_id=1, replica_groups=mesh['rows'=16,'cols'=16] {'rows','cols'}, use_global_device_ids=true, to_apply=%region_43.49 | all-reduce | flops 64 | bytes 512 | tf_op jit(solution)/shard_map/psum | solution.py:24
  2155.0 74.7 %psum.291 = f32[64,64]{0,1:T(8,128)S(1)} all-reduce(f32[64,64]{0,1:T(8,128)S(1)} %fusion.140), channel_id=1, replica_groups=mesh['rows'=16,'cols'=16] {'rows','cols'}, use_global_device_ids=true, to_apply=%region_44.50 | all-reduce | flops 4096 | bytes 32768 | tf_op jit(solution)/shard_map/psum | solution.py:27
  2229.8 5.8 cholesky.382
  2244.6 43.4 %psum.292 = f32[128,64]{0,1:T(8,128)S(1)} all-reduce(f32[128,64]{0,1:T(8,128)S(1)} %bitcast.458), channel_id=1, replica_groups=mesh['rows'=16,'cols'=16] {'rows'}, use_global_device_ids=true, to_apply=%region_45.51 | all-reduce | flops 8192 | bytes 65536 | tf_op jit(solution)/shard_map/psum | solution.py:73
  2288.5 76.4 %psum.293 = f32[64]{0:T(128)S(1)} all-reduce(f32[64]{0:T(128)S(1)} %multiply_reduce_fusion), channel_id=1, replica_groups=mesh['rows'=16,'cols'=16] {'rows','cols'}, use_global_device_ids=true, to_apply=%region_47.53 | all-reduce | flops 64 | bytes 512 | tf_op jit(solution)/shard_map/psum | solution.py:24
  2367.5 73.9 %all-reduce = (f32[32,64]{0,1:T(8,128)S(1)}, f32[64,64]{0,1:T(8,128)S(1)}) all-reduce(f32[32,64]{0,1:T(8,128)S(1)} %bitcast.448, f32[64,64]{0,1:T(8,128)S(1)} %fusion.138), channel_id=1, replica_groups=mesh['rows'=16,'cols'=16] {'rows','cols'}, use_global_device_ids=true, to_apply=%region_49.55 | all-reduce | flops 6144 | bytes 49152 | tf_op jit(solution)/shard_map/psum | solution.py:82
  2441.5 5.8 cholesky.393
  (209 shorter events, 151.8 us)
Async XLA Ops:
  0.6 170.5 %copy-start = (f32[32,128,128]{2,1,0:T(8,128)S(1)}, f32[32,128,128]{2,1,0:T(8,128)}, u32[]{:S(2)}) copy-start(f32[32,128,128]{2,1,0:T(8,128)} %param.12) | copy-start | bytes 6291460
  2155.0 89.7 %copy-start.1 = (f32[128,64]{0,1:T(8,128)}, f32[128,64]{0,1:T(8,128)S(1)}, u32[]{:S(2)}) copy-start(f32[128,64]{0,1:T(8,128)S(1)} %broadcast_divide_fusion.1) | copy-start | bytes 98308
  2365.3 89.4 %copy-start.2 = (f32[128,64]{0,1:T(8,128)}, f32[128,64]{0,1:T(8,128)S(1)}, u32[]{:S(2)}) copy-start(f32[128,64]{0,1:T(8,128)S(1)} %broadcast_divide_fusion) | copy-start | bytes 98308
where the time goes:
time: 2470 us; the launch traced here: 2460 us
  blocking collectives  2210 us (89%)
  other arithmetic  185 us (7%)
  matrix products  57.5 us (2%)
    psum x11, blocking collectives, settle(): squares = lax.psum(jnp.sum(raw_share * raw_share, axis=0), ('rows', 'cols'))  891 us
    psum x6, blocking collectives, settle(): gram_whole = lax.psum(gram_local(normed), ('rows', 'cols'))  446 us
    psum x5, blocking collectives, per_device(): summed_third = lax.psum(outgoing, ('rows', 'cols'))  371 us
    psum x5, blocking collectives, per_device(): mttkrp_first = lax.psum(partial_first, 'cols')  284 us
    psum x5, blocking collectives, per_device(): summed_second = lax.psum(outgoing, 'rows')  218 us
    another operation x45, other arithmetic, solve_right(): cholesky_low = jnp.linalg.cholesky(system)  97.8 us
    another operation x30, other arithmetic, solve_right(): lax.linalg.triangular_solve(cholesky_low, halfway, left_side=False, lower...  83.2 us

commit v1 on v0

--- a/solution.py
+++ b/solution.py
@@ -70,7 +70,7 @@
         )
         partial_second = jnp.einsum("rkj,kr->jr", contract_second, third, precision=HIGHEST)
         outgoing = partial_second
-        summed_second = lax.psum(outgoing, "rows")
+        summed_second = jnp.sum(lax.all_gather(outgoing, "rows"), axis=0)
         first = carried_first
         system_second = gram_third * gram_first
         raw_block = solve_right(summed_second, system_second)

time: 2470 us -> 2330 us (0.943)
  blocking collectives: 2210 us -> 2070 us
    psum x5 -> x0, blocking collectives: 218 us -> none  [per_device(): summed_second = lax.psum(outgoing, 'rows')]
    all_gather x0 -> x5, blocking collectives: none -> 87.2 us  [per_device(): summed_second = jnp.sum(lax.all_gather(outgoing, 'rows'), axis=0)]
where the time goes in v1:
time: 2330 us; the launch traced here: 2310 us
  blocking collectives  2070 us (89%)
  other arithmetic  185 us (8%)
  matrix products  57.5 us (2%)
    psum x11, blocking collectives, settle(): squares = lax.psum(jnp.sum(raw_share * raw_share, axis=0), ('rows', 'cols'))  873 us
    psum x6, blocking collectives, settle(): gram_whole = lax.psum(gram_local(normed), ('rows', 'cols'))  446 us
    psum x5, blocking collectives, per_device(): summed_third = lax.psum(outgoing, ('rows', 'cols'))  374 us
    psum x5, blocking collectives, per_device(): mttkrp_first = lax.psum(partial_first, 'cols')  288 us
    another operation x45, other arithmetic, solve_right(): cholesky_low = jnp.linalg.cholesky(system)  97.8 us
    all_gather x5, blocking collectives, per_device(): summed_second = jnp.sum(lax.all_gather(outgoing, 'rows'), axis=0)  87.2 us
    another operation x30, other arithmetic, solve_right(): lax.linalg.triangular_solve(cholesky_low, halfway, left_side=False, lower...  83.2 us

profile of v1, /device:TPU:1, one launch (start us, length us, event | category | flops | bytes accessed | tf_op | source)
XLA Modules:
  0.0 2314.8 jit_solution(11819328879103933585)
XLA Ops:
  1.7 81.4 %psum.224 = f32[64]{0:T(128)S(1)} all-reduce(f32[64]{0:T(128)S(1)} %multiply_reduce_fusion.10), channel_id=1, replica_groups=mesh['rows'=16,'cols'=16] {'rows','cols'}, use_global_device_ids=true, to_apply=%region_1.0 | all-reduce | flops 64 | bytes 512 | tf_op jit(solution)/shard_map/psum | solution.py:24
  85.1 72.8 %psum.225 = f32[64,64]{0,1:T(8,128)S(1)} all-reduce(f32[64,64]{0,1:T(8,128)S(1)} %fusion.163), channel_id=1, replica_groups=mesh['rows'=16,'cols'=16] {'rows','cols'}, use_global_device_ids=true, to_apply=%region_2.0 | all-reduce | flops 4096 | bytes 32768 | tf_op jit(solution)/shard_map/psum | solution.py:27
  159.0 5.8 cholesky.239
  166.2 4.9 custom-call.41
  175.8 56.8 %psum.226 = f32[128,64]{0,1:T(8,128)S(1)} all-reduce(f32[128,64]{0,1:T(8,128)S(1)} %bitcast.484), channel_id=1, replica_groups=mesh['rows'=16,'cols'=16] {'cols'}, use_global_device_ids=true, to_apply=%region_5.0 | all-reduce | flops 8192 | bytes 65536 | tf_op jit(solution)/shard_map/psum | solution.py:58
  233.2 86.1 %psum.227 = f32[64]{0:T(128)S(1)} all-reduce(f32[64]{0:T(128)S(1)} %multiply_reduce_fusion.9), channel_id=1, replica_groups=mesh['rows'=16,'cols'=16] {'rows','cols'}, use_global_device_ids=true, to_apply=%region_7.11 | all-reduce | flops 64 | bytes 512 | tf_op jit(solution)/shard_map/psum | solution.py:24
  319.6 73.9 %psum.228 = f32[64,64]{0,1:T(8,128)S(1)} all-reduce(f32[64,64]{0,1:T(8,128)S(1)} %fusion.160), channel_id=1, replica_groups=mesh['rows'=16,'cols'=16] {'rows','cols'}, use_global_device_ids=true, to_apply=%region_8.12 | all-reduce | flops 4096 | bytes 32768 | tf_op jit(solution)/shard_map/psum | solution.py:27
  393.6 5.8 cholesky.250
  408.5 18.1 all-gather
  427.4 73.4 %psum.229 = f32[64]{0:T(128)S(1)} all-reduce(f32[64]{0:T(128)S(1)} %multiply_reduce_fusion.8), channel_id=1, replica_groups=mesh['rows'=16,'cols'=16] {'rows','cols'}, use_global_device_ids=true, to_apply=%region_11.15 | all-reduce | flops 64 | bytes 512 | tf_op jit(solution)/shard_map/psum | solution.py:24
  503.4 74.8 %all-reduce.4 = (f32[32,64]{0,1:T(8,128)S(1)}, f32[64,64]{0,1:T(8,128)S(1)}) all-reduce(f32[32,64]{0,1:T(8,128)S(1)} %bitcast.479, f32[64,64]{0,1:T(8,128)S(1)} %fusion.157), channel_id=1, replica_groups=mesh['rows'=16,'cols'=16] {'rows','cols'}, use_global_device_ids=true, to_apply=%region_13.17 | all-reduce | flops 6144 | bytes 49152 | tf_op jit(solution)/shard_map/psum | solution.py:82
  578.2 5.8 cholesky.261
  591.2 5.8 cholesky.272
  607.2 57.7 %psum.232 = f32[128,64]{0,1:T(8,128)S(1)} all-reduce(f32[128,64]{0,1:T(8,128)S(1)} %bitcast.485), channel_id=1, replica_groups=mesh['rows'=16,'cols'=16] {'cols'}, use_global_device_ids=true, to_apply=%region_14.20 | all-reduce | flops 8192 | bytes 65536 | tf_op jit(solution)/shard_map/psum | solution.py:58
  665.5 84.6 %psum.233 = f32[64]{0:T(128)S(1)} all-reduce(f32[64]{0:T(128)S(1)} %multiply_reduce_fusion.7), channel_id=1, replica_groups=mesh['rows'=16,'cols'=16] {'rows','cols'}, use_global_device_ids=true, to_apply=%region_16.22 | all-reduce | flops 64 | bytes 512 | tf_op jit(solution)/shard_map/psum | solution.py:24
  750.4 74.9 %psum.234 = f32[64,64]{0,1:T(8,128)S(1)} all-reduce(f32[64,64]{0,1:T(8,128)S(1)} %fusion.155), channel_id=1, replica_groups=mesh['rows'=16,'cols'=16] {'rows','cols'}, use_global_device_ids=true, to_apply=%region_17.23 | all-reduce | flops 4096 | bytes 32768 | tf_op jit(solution)/shard_map/psum | solution.py:27
  825.4 5.8 cholesky.283
  840.2 17.3 all-gather.1
  858.3 73.4 %psum.235 = f32[64]{0:T(128)S(1)} all-reduce(f32[64]{0:T(128)S(1)} %multiply_reduce_fusion.6), channel_id=1, replica_groups=mesh['rows'=16,'cols'=16] {'rows','cols'}, use_global_device_ids=true, to_apply=%region_20.26 | all-reduce | flops 64 | bytes 512 | tf_op jit(solution)/shard_map/psum | solution.py:24
  934.3 74.7 %all-reduce.3 = (f32[32,64]{0,1:T(8,128)S(1)}, f32[64,64]{0,1:T(8,128)S(1)}) all-reduce(f32[32,64]{0,1:T(8,128)S(1)} %bitcast.480, f32[64,64]{0,1:T(8,128)S(1)} %fusion.152), channel_id=1, replica_groups=mesh['rows'=16,'cols'=16] {'rows','cols'}, use_global_device_ids=true, to_apply=%region_22.28 | all-reduce | flops 6144 | bytes 49152 | tf_op jit(solution)/shard_map/psum | solution.py:82
  1009.1 5.8 cholesky.294
  1022.1 5.8 cholesky.305
  1038.1 57.7 %psum.238 = f32[128,64]{0,1:T(8,128)S(1)} all-reduce(f32[128,64]{0,1:T(8,128)S(1)} %bitcast.486), channel_id=1, replica_groups=mesh['rows'=16,'cols'=16] {'cols'}, use_global_device_ids=true, to_apply=%region_23.29 | all-reduce | flops 8192 | bytes 65536 | tf_op jit(solution)/shard_map/psum | solution.py:58
  1096.4 84.6 %psum.239 = f32[64]{0:T(128)S(1)} all-reduce(f32[64]{0:T(128)S(1)} %multiply_reduce_fusion.5), channel_id=1, replica_groups=mesh['rows'=16,'cols'=16] {'rows','cols'}, use_global_device_ids=true, to_apply=%region_25.31 | all-reduce | flops 64 | bytes 512 | tf_op jit(solution)/shard_map/psum | solution.py:24
  1181.3 74.7 %psum.240 = f32[64,64]{0,1:T(8,128)S(1)} all-reduce(f32[64,64]{0,1:T(8,128)S(1)} %fusion.150), channel_id=1, replica_groups=mesh['rows'=16,'cols'=16] {'rows','cols'}, use_global_device_ids=true, to_apply=%region_26.32 | all-reduce | flops 4096 | bytes 32768 | tf_op jit(solution)/shard_map/psum | solution.py:27
  1256.0 5.8 cholesky.316
  1270.8 17.3 all-gather.2
  1288.9 73.5 %psum.241 = f32[64]{0:T(128)S(1)} all-reduce(f32[64]{0:T(128)S(1)} %multiply_reduce_fusion.4), channel_id=1, replica_groups=mesh['rows'=16,'cols'=16] {'rows','cols'}, use_global_device_ids=true, to_apply=%region_29.35 | all-reduce | flops 64 | bytes 512 | tf_op jit(solution)/shard_map/psum | solution.py:24
  1364.9 75.0 %all-reduce.2 = (f32[32,64]{0,1:T(8,128)S(1)}, f32[64,64]{0,1:T(8,128)S(1)}) all-reduce(f32[32,64]{0,1:T(8,128)S(1)} %bitcast.481, f32[64,64]{0,1:T(8,128)S(1)} %fusion.147), channel_id=1, replica_groups=mesh['rows'=16,'cols'=16] {'rows','cols'}, use_global_device_ids=true, to_apply=%region_31.37 | all-reduce | flops 6144 | bytes 49152 | tf_op jit(solution)/shard_map/psum | solution.py:82
  1440.0 5.8 cholesky.327
  1453.0 5.8 cholesky.338
  1468.9 57.7 %psum.244 = f32[128,64]{0,1:T(8,128)S(1)} all-reduce(f32[128,64]{0,1:T(8,128)S(1)} %bitcast.487), channel_id=1, replica_groups=mesh['rows'=16,'cols'=16] {'cols'}, use_global_device_ids=true, to_apply=%region_32.38 | all-reduce | flops 8192 | bytes 65536 | tf_op jit(solution)/shard_map/psum | solution.py:58
  1527.2 84.6 %psum.245 = f32[64]{0:T(128)S(1)} all-reduce(f32[64]{0:T(128)S(1)} %multiply_reduce_fusion.3), channel_id=1, replica_groups=mesh['rows'=16,'cols'=16] {'rows','cols'}, use_global_device_ids=true, to_apply=%region_34.40 | all-reduce | flops 64 | bytes 512 | tf_op jit(solution)/shard_map/psum | solution.py:24
  1612.1 74.6 %psum.246 = f32[64,64]{0,1:T(8,128)S(1)} all-reduce(f32[64,64]{0,1:T(8,128)S(1)} %fusion.145), channel_id=1, replica_groups=mesh['rows'=16,'cols'=16] {'rows','cols'}, use_global_device_ids=true, to_apply=%region_35.41 | all-reduce | flops 4096 | bytes 32768 | tf_op jit(solution)/shard_map/psum | solution.py:27
  1686.8 5.8 cholesky.349
  1701.6 17.3 all-gather.3
  1719.7 73.5 %psum.247 = f32[64]{0:T(128)S(1)} all-reduce(f32[64]{0:T(128)S(1)} %multiply_reduce_fusion.2), channel_id=1, replica_groups=mesh['rows'=16,'cols'=16] {'rows','cols'}, use_global_device_ids=true, to_apply=%region_38.44 | all-reduce | flops 64 | bytes 512 | tf_op jit(solution)/shard_map/psum | solution.py:24
  1795.7 74.8 %all-reduce.1 = (f32[32,64]{0,1:T(8,128)S(1)}, f32[64,64]{0,1:T(8,128)S(1)}) all-reduce(f32[32,64]{0,1:T(8,128)S(1)} %bitcast.482, f32[64,64]{0,1:T(8,128)S(1)} %fusion.142), channel_id=1, replica_groups=mesh['rows'=16,'cols'=16] {'rows','cols'}, use_global_device_ids=true, to_apply=%region_40.46 | all-reduce | flops 6144 | bytes 49152 | tf_op jit(solution)/shard_map/psum | solution.py:82
  1870.6 5.8 cholesky.360
  1883.6 5.8 cholesky.371
  1899.5 57.7 %psum.250 = f32[128,64]{0,1:T(8,128)S(1)} all-reduce(f32[128,64]{0,1:T(8,128)S(1)} %bitcast.488), channel_id=1, replica_groups=mesh['rows'=16,'cols'=16] {'cols'}, use_global_device_ids=true, to_apply=%region_41.47 | all-reduce | flops 8192 | bytes 65536 | tf_op jit(solution)/shard_map/psum | solution.py:58
  1957.8 84.6 %psum.251 = f32[64]{0:T(128)S(1)} all-reduce(f32[64]{0:T(128)S(1)} %multiply_reduce_fusion.1), channel_id=1, replica_groups=mesh['rows'=16,'cols'=16] {'rows','cols'}, use_global_device_ids=true, to_apply=%region_43.49 | all-reduce | flops 64 | bytes 512 | tf_op jit(solution)/shard_map/psum | solution.py:24
  2042.8 74.7 %psum.252 = f32[64,64]{0,1:T(8,128)S(1)} all-reduce(f32[64,64]{0,1:T(8,128)S(1)} %fusion.140), channel_id=1, replica_groups=mesh['rows'=16,'cols'=16] {'rows','cols'}, use_global_device_ids=true, to_apply=%region_44.50 | all-reduce | flops 4096 | bytes 32768 | tf_op jit(solution)/shard_map/psum | solution.py:27
  2117.6 5.8 cholesky.382
  2132.4 17.3 all-gather.4
  2150.5 73.5 %psum.253 = f32[64]{0:T(128)S(1)} all-reduce(f32[64]{0:T(128)S(1)} %multiply_reduce_fusion), channel_id=1, replica_groups=mesh['rows'=16,'cols'=16] {'rows','cols'}, use_global_device_ids=true, to_apply=%region_47.53 | all-reduce | flops 64 | bytes 512 | tf_op jit(solution)/shard_map/psum | solution.py:24
  2226.5 74.5 %all-reduce = (f32[32,64]{0,1:T(8,128)S(1)}, f32[64,64]{0,1:T(8,128)S(1)}) all-reduce(f32[32,64]{0,1:T(8,128)S(1)} %bitcast.483, f32[64,64]{0,1:T(8,128)S(1)} %fusion.138), channel_id=1, replica_groups=mesh['rows'=16,'cols'=16] {'rows','cols'}, use_global_device_ids=true, to_apply=%region_49.55 | all-reduce | flops 6144 | bytes 49152 | tf_op jit(solution)/shard_map/psum | solution.py:82
  2301.2 5.8 cholesky.393
  (219 shorter events, 152.7 us)
Async XLA Ops:
  0.6 170.5 %copy-start = (f32[32,128,128]{2,1,0:T(8,128)S(1)}, f32[32,128,128]{2,1,0:T(8,128)}, u32[]{:S(2)}) copy-start(f32[32,128,128]{2,1,0:T(8,128)} %param.12) | copy-start | bytes 6291460
  2042.8 89.6 %copy-start.1 = (f32[128,64]{0,1:T(8,128)}, f32[128,64]{0,1:T(8,128)S(1)}, u32[]{:S(2)}) copy-start(f32[128,64]{0,1:T(8,128)S(1)} %broadcast_divide_fusion.1) | copy-start | bytes 98308
  2224.3 90.0 %copy-start.2 = (f32[128,64]{0,1:T(8,128)}, f32[128,64]{0,1:T(8,128)S(1)}, u32[]{:S(2)}) copy-start(f32[128,64]{0,1:T(8,128)S(1)} %broadcast_divide_fusion) | copy-start | bytes 98308
